TPU v7x, 32 devices: a whole 2x2x4 slice. The times are simulated.
32 devices in a mesh: row: 8 (over y, x, core), col: 4 (over z).
Axes of the slice: x: 2, y: 2, z: 4, core: 2. Of those that a mesh axis runs over, the one named last changes fastest.
Arguments:
- left_act: bfloat16 [32, 64, 256], P(None, 'col', 'row'), may hold values from -6 to 6
- right_act: bfloat16 [32, 64, 256], P(None, 'row', 'col'), may hold values from -6 to 6
- cotangent: bfloat16 [256, 256, 128], P('row', 'col'), may hold values from -4 to 4
- weight: bfloat16 [1024, 128], replicated, may hold values from -0.1875 to 0.1875
Outputs:
- grad_left: float32 [32, 64, 256], P(None, 'col', 'row')
- grad_right: float32 [32, 64, 256], P(None, 'row', 'col')
- grad_weight: float32 [1024, 128], P('row')
All inputs are finite; a program needn't handle non-finite values.
Results may differ from a plain program's by a relative error of at most 0.0029.
Values may be sent and summed in bfloat16 or wider, within the bound.
No kernel may reach another device: no remote copies, remote signals or barrier semaphores. Data moves between devices by JAX's collectives and lax.ppermute only.
A program may use at most 128 MiB of HBM per device.

v0:
```python
import jax
import jax.numpy as jnp
from jax import lax
from jax.sharding import PartitionSpec as P

S = 64


def body(left_act, right_act, cotangent, weight):
    left = lax.all_gather(left_act, "col", axis=1, tiled=True)
    right = lax.all_gather(right_act, "row", axis=1, tiled=True)
    first, second = (cotangent.shape[0], cotangent.shape[1])
    chans = left.shape[0]
    outer = (
        jnp.einsum("csi,dsj->ijcd", left, right, preferred_element_type=jnp.float32) / S
    ).astype(jnp.bfloat16)
    outer_flat = outer.reshape(first * second, chans * chans)
    grad_flat = cotangent.reshape(first * second, cotangent.shape[2])
    contract = (((0,), (0,)), ((), ()))
    partial_w = lax.dot_general(outer_flat, grad_flat, contract, preferred_element_type=jnp.float32)
    own_rows = lax.psum_scatter(partial_w, "row", scatter_dimension=0, tiled=True)
    grad_weight = lax.psum(own_rows, "col")
    grad_outer = lax.dot_general(
        grad_flat, weight, (((1,), (1,)), ((), ())), preferred_element_type=jnp.float32
    )
    grad_outer = grad_outer.astype(jnp.bfloat16).reshape(first, second, chans, chans)
    left_part = (
        jnp.einsum("ijcd,dsj->csi", grad_outer, right, preferred_element_type=jnp.float32) / S
    )
    right_part = (
        jnp.einsum("ijcd,csi->dsj", grad_outer, left, preferred_element_type=jnp.float32) / S
    )
    grad_left = lax.psum_scatter(left_part, "col", scatter_dimension=1, tiled=True)
    grad_right = lax.psum_scatter(right_part, "row", scatter_dimension=1, tiled=True)
    return (grad_left, grad_right, grad_weight)


def solution(mesh):
    return jax.shard_map(
        body,
        mesh=mesh,
        in_specs=(P(None, "col", "row"), P(None, "row", "col"), P("row", "col", None), P()),
        out_specs=(P(None, "col", "row"), P(None, "row", "col"), P("row", None)),
        check_vma=False,
    )
```

profile of v0, /device:TPU:0, one launch (start us, length us, event | category | flops | bytes accessed | tf_op | source)
XLA Modules:
  0.0 213.5 jit_solution(4263041880610660756)
XLA Ops:
  7.2 0.0 copy-start
  7.2 0.0 reduce-scatter.8.cloned.1.call-start
  7.2 17.7 %all_gather.7 = bf16[32,64,32]{2,1,0:T(8,128)(2,1)S(1)} all-gather(bf16[32,16,32]{2,1,0:T(8,128)(2,1)} %param.4), channel_id=1, replica_groups=mesh['row'=8,'col'=4] {'col'}, dimensions={1}, use_global_device_ids=true | all-gather | bytes 163840 | tf_op jit(solution)/shard_map/all_gather | solution.py:10
  24.9 10.3 %all_gather.6 = bf16[32,64,64]{2,1,0:T(8,128)(2,1)S(1)} all-gather(bf16[32,8,64]{2,1,0:T(8,128)(2,1)} %param.5), channel_id=1, replica_groups=mesh['row'=8,'col'=4] {'row'}, dimensions={1}, use_global_device_ids=true | all-gather | bytes 294912 | tf_op jit(solution)/shard_map/all_gather | solution.py:11
  35.2 5.6 %fusion = bf16[32,64,32,32]{1,0,2,3:T(8,128)(2,1)} fusion(bf16[32,64,64]{2,1,0:T(8,128)(2,1)S(1)} %all_gather.6, bf16[32,64,32]{2,1,0:T(8,128)(2,1)S(1)} %all_gather.7), kind=kOutput, calls=%fused_computation.1 | convolution fusion | flops 272629760 | bytes 4587520 | tf_op jit(solution)/shard_map/csi,dsj->ijcd/dot_general | solution.py:15
  40.8 9.1 %copy.20 = bf16[32,64,32,32]{1,0,3,2:T(8,128)(2,1)} copy(bf16[32,64,32,32]{1,0,2,3:T(8,128)(2,1)} %fusion) | data formatting | bytes 8388608 | tf_op jit(solution)/shard_map/convert_element_type | solution.py:16
  49.9 0.0 copy-start.1
  49.9 12.4 %reshape.17 = bf16[2048,1024]{0,1:T(8,128)(2,1)} reshape(bf16[32,64,32,32]{1,0,3,2:T(8,128)(2,1)} %copy.20) | data formatting | bytes 8388608 | tf_op jit(solution)/shard_map/reshape | solution.py:17
  62.3 0.0 copy-done
  62.3 4.3 %fusion.9 = f32[1024,128]{1,0:T(8,128)} fusion(bf16[2048,1024]{0,1:T(8,128)(2,1)} %reshape.17, bf16[2048,128]{1,0:T(8,128)(2,1)S(1)} %bitcast.47), kind=kOutput, calls=%fused_computation.13 | convolution fusion | flops 536870912 | bytes 5242880 | tf_op jit(solution)/shard_map/dot_general | solution.py:20
  66.6 0.0 reduce-scatter.8.cloned.1.call-update
  66.6 0.0 reduce-scatter.4.cloned.1.call-start
  66.6 0.0 copy-done.1
  66.7 3.2 %convolution_convert_fusion = bf16[2048,1024]{1,0:T(8,128)(2,1)} fusion(bf16[2048,128]{1,0:T(8,128)(2,1)S(1)} %bitcast.46, bf16[1024,128]{1,0:T(8,128)(2,1)S(1)} %copy-done.1), kind=kOutput, calls=%fused_computation.2 | convolution fusion | flops 538968064 | bytes 4980736 | tf_op jit(solution)/shard_map/dot_general | solution.py:23
  69.8 6.5 %copy.17 = bf16[2048,1024]{0,1:T(8,128)(2,1)} copy(bf16[2048,1024]{1,0:T(8,128)(2,1)} %convolution_convert_fusion) | data formatting | bytes 8388608 | tf_op jit(solution)/shard_map/convert_element_type | solution.py:26
  76.3 12.9 %reshape.16 = bf16[32,64,32,32]{1,0,3,2:T(8,128)(2,1)} reshape(bf16[2048,1024]{0,1:T(8,128)(2,1)} %copy.17) | data formatting | bytes 8388608 | tf_op jit(solution)/shard_map/reshape | solution.py:26
  89.2 5.7 %fusion.4 = f32[32,64,32]{1,2,0:T(8,128)S(1)} fusion(bf16[32,64,32,32]{1,0,3,2:T(8,128)(2,1)} %reshape.16, bf16[32,64,64]{2,1,0:T(8,128)(2,1)S(1)} %all_gather.6), kind=kOutput, calls=%fused_computation.8 | convolution fusion | flops 268500992 | bytes 4718592 | tf_op jit(solution)/shard_map/ijcd,dsj->csi/dot_general | solution.py:28
  95.0 1.8 copy.18
  96.8 0.0 reduce-scatter.4.cloned.1.call-update
  96.8 0.2 reduce-scatter.6.cloned.1.call-start
  97.1 7.0 %fusion.2 = f32[32,64,64]{1,2,0:T(8,128)S(1)} fusion(bf16[32,64,32,32]{1,0,3,2:T(8,128)(2,1)} %reshape.16, bf16[32,64,32]{2,1,0:T(8,128)(2,1)S(1)} %all_gather.7), kind=kOutput, calls=%fused_computation.5 | convolution fusion | flops 268566528 | bytes 4849664 | tf_op jit(solution)/shard_map/ijcd,csi->dsj/dot_general | solution.py:31
  104.1 1.8 copy.19
  105.9 0.0 reduce-scatter.6.cloned.1.call-update
  105.9 0.0 all-reduce.2.cloned.1.call-start
  105.9 0.0 reduce-scatter.8.cloned.1.call-done
  106.0 0.5 all-reduce.2.cloned.1.call-update
  106.5 24.8 %reduce-scatter.4.cloned.1.call-done = f32[32,16,32]{2,0,1:T(8,128)} async-done(((f32[32,64,32]{2,0,1:T(8,128)}), f32[32,16,32]{2,0,1:T(8,128)}) %reduce-scatter.4.cloned.1.call-update) | async-done | bytes 65552 | tf_op jit(solution)/shard_map/reduce_scatter | solution.py:33
  131.3 1.8 copy.21
  133.1 35.9 %reduce-scatter.6.cloned.1.call-done = f32[32,8,64]{2,0,1:T(8,128)} async-done(((f32[32,64,64]{2,0,1:T(8,128)}), f32[32,8,64]{2,0,1:T(8,128)}) %reduce-scatter.6.cloned.1.call-update) | async-done | bytes 65552 | tf_op jit(solution)/shard_map/reduce_scatter | solution.py:34
  169.0 1.6 copy.22
  170.6 34.9 %all-reduce.2.cloned.1.call-done = f32[128,128]{1,0:T(8,128)} async-done(((f32[128,128]{1,0:T(8,128)}), f32[128,128]{1,0:T(8,128)}) %all-reduce.2.cloned.1.call-update) | async-done | bytes 65552 | tf_op jit(solution)/shard_map/psum | solution.py:22
  205.5 1.5 copy.27
Async XLA Ops:
  7.2 55.2 %copy-start = (bf16[32,64,128]{2,1,0:T(8,128)(2,1)S(1)}, bf16[32,64,128]{2,1,0:T(8,128)(2,1)}, u32[]{:S(2)}) copy-start(bf16[32,64,128]{2,1,0:T(8,128)(2,1)} %param.6) | copy-start | bytes 1572868
  7.2 98.8 %reduce-scatter.8.cloned.1.call-start = ((), (), s32[]{:S(2)}) async-start(), calls=%async_computation.5 | async-start | bytes 589824 | tf_op jit(solution)/shard_map/reduce_scatter | solution.py:21
  49.9 16.7 %copy-start.1 = (bf16[1024,128]{1,0:T(8,128)(2,1)S(1)}, bf16[1024,128]{1,0:T(8,128)(2,1)}, u32[]{:S(2)}) copy-start(bf16[1024,128]{1,0:T(8,128)(2,1)} %param.7) | copy-start | bytes 786436
  66.6 64.7 %reduce-scatter.4.cloned.1.call-start = ((), (), s32[]{:S(2)}) async-start(), calls=%async_computation.3 | async-start | bytes 1310720 | tf_op jit(solution)/shard_map/reduce_scatter | solution.py:33
  96.8 72.1 %reduce-scatter.6.cloned.1.call-start = ((), (), s32[]{:S(2)}) async-start(), calls=%async_computation.4 | async-start | bytes 1179648 | tf_op jit(solution)/shard_map/reduce_scatter | solution.py:34
  105.9 99.6 %all-reduce.2.cloned.1.call-start = ((), (), s32[]{:S(2)}) async-start(), calls=%async_computation.6 | async-start | bytes 131072 | tf_op jit(solution)/shard_map/psum | solution.py:22
Sparse Core Ops, SparseCore 0:
  66.7 34.8 reduce-scatter.7
  103.9 27.3 reduce-scatter.3
  134.5 34.4 reduce-scatter.5
  171.1 34.2 all-reduce.1
where the time goes:
time: 215 us; the launch traced here: 213 us
  waiting for transfers between devices  96.1 us (45%)
  local copies, waits for them, and re-layouts  49.4 us (23%)
  blocking collectives  28 us (13%)
  matrix products  25.8 us (12%)
  between operations  13.8 us (6%)
    reduce_scatter x1, waiting for transfers between devices, body(): lax.psum_scatter(right_part, 'row', scatter_dimension=1, tiled=True)  35.9 us
    psum x1, waiting for transfers between devices, body(): grad_weight = lax.psum(own_rows, 'col')  34.9 us
    reduce_scatter x1, waiting for transfers between devices, body(): lax.psum_scatter(left_part, 'col', scatter_dimension=1, tiled=True)  24.8 us
    all_gather x1, blocking collectives, body(): left = lax.all_gather(left_act, 'col', axis=1, tiled=True)  17.7 us
    reshape x1, local copies, waits for them, and re-layouts, body(): grad_outer.astype(jnp.bfloat16).reshape(first, second, chans, chans)  12.9 us
    reshape x1, local copies, waits for them, and re-layouts, body(): outer_flat = outer.reshape(first * second, chans * chans)  12.4 us
    all_gather x1, blocking collectives, body(): right = lax.all_gather(right_act, 'row', axis=1, tiled=True)  10.3 us
    convert_element_type x1, local copies, waits for them, and re-layouts, body(): outer = (jnp.einsum('csi,dsj->ijcd', left, right, preferred_element_type=...  9.13 us
  transfers between devices with their start and end apart: 4, of which 3 were waited for; matrix products, arithmetic and copies ran while one was open for 20% of the time, Pallas kernels for 0%

commit v1 on v0

--- a/solution.py
+++ b/solution.py
@@ -19,7 +19,7 @@
     contract = (((0,), (0,)), ((), ()))
     partial_w = lax.dot_general(outer_flat, grad_flat, contract, preferred_element_type=jnp.float32)
     own_rows = lax.psum_scatter(partial_w, "row", scatter_dimension=0, tiled=True)
-    grad_weight = lax.psum(own_rows, "col")
+    grad_weight = jnp.sum(lax.all_gather(own_rows, "col"), axis=0)
     grad_outer = lax.dot_general(
         grad_flat, weight, (((1,), (1,)), ((), ())), preferred_element_type=jnp.float32
     )

time: 215 us -> 185 us (0.86)
  waiting for transfers between devices: 96.1 us -> 46.6 us
  blocking collectives: 28 us -> 48.2 us
    psum x1 -> x0, waiting for transfers between devices: 34.9 us -> none  [body(): grad_weight = lax.psum(own_rows, 'col')]
    reduce_scatter x1, waiting for transfers between devices: 24.8 us -> 0.02 us  [body(): lax.psum_scatter(left_part, 'col', scatter_dimension=1, tiled=True)]
    reduce_scatter x1, waiting for transfers between devices: 0.02 us -> 22.1 us  [body(): lax.psum_scatter(partial_w, 'row', scatter_dimension=0, tiled=True)]
    all_gather x0 -> x1, blocking collectives: none -> 14.1 us  [body(): grad_weight = jnp.sum(lax.all_gather(own_rows, 'col'), axis=0)]
    reduce_scatter x1, waiting for transfers between devices: 35.9 us -> 24.4 us  [body(): lax.psum_scatter(right_part, 'row', scatter_dimension=1, tiled=True)]
    all_gather x1, blocking collectives: 17.7 us -> 22.2 us  [body(): left = lax.all_gather(left_act, 'col', axis=1, tiled=True)]
    unnamed x7 -> x6, local copies, waits for them, and re-layouts: 4.93 us -> 3.47 us
  transfers between devices with their start and end apart: 4 -> 3, of which waited for: 3 -> 2; matrix products, arithmetic and copies ran while one was open for 20% -> 23% of each run, Pallas kernels for 0% -> 0%
where the time goes in v1:
time: 185 us; the launch traced here: 184 us
  blocking collectives  48.2 us (26%)
  local copies, waits for them, and re-layouts  47.9 us (26%)
  waiting for transfers between devices  46.6 us (25%)
  matrix products  26.7 us (14%)
  between operations  13.8 us (7%)
    reduce_scatter x1, waiting for transfers between devices, body(): lax.psum_scatter(right_part, 'row', scatter_dimension=1, tiled=True)  24.4 us
    all_gather x1, blocking collectives, body(): left = lax.all_gather(left_act, 'col', axis=1, tiled=True)  22.2 us
    reduce_scatter x1, waiting for transfers between devices, body(): lax.psum_scatter(partial_w, 'row', scatter_dimension=0, tiled=True)  22.1 us
    all_gather x1, blocking collectives, body(): grad_weight = jnp.sum(lax.all_gather(own_rows, 'col'), axis=0)  14.1 us
    reshape x1, local copies, waits for them, and re-layouts, body(): grad_outer.astype(jnp.bfloat16).reshape(first, second, chans, chans)  12.9 us
    reshape x1, local copies, waits for them, and re-layouts, body(): outer_flat = outer.reshape(first * second, chans * chans)  12.3 us
    all_gather x1, blocking collectives, body(): right = lax.all_gather(right_act, 'row', axis=1, tiled=True)  11.9 us
    convert_element_type x1, local copies, waits for them, and re-layouts, body(): outer = (jnp.einsum('csi,dsj->ijcd', left, right, preferred_element_type=...  9.17 us
  transfers between devices with their start and end apart: 3, of which 2 were waited for; matrix products, arithmetic and copies ran while one was open for 23% of the time, Pallas kernels for 0%

profile of v1, /device:TPU:0, one launch (start us, length us, event | category | flops | bytes accessed | tf_op | source)
XLA Modules:
  0.0 184.1 jit_solution(14907400142397622416)
XLA Ops:
  7.2 0.0 copy-start
  7.2 0.0 reduce-scatter.4.cloned.1.call-start
  7.2 11.9 %all_gather.12 = bf16[32,64,64]{2,1,0:T(8,128)(2,1)S(1)} all-gather(bf16[32,8,64]{2,1,0:T(8,128)(2,1)} %param.5), channel_id=1, replica_groups=mesh['row'=8,'col'=4] {'row'}, dimensions={1}, use_global_device_ids=true | all-gather | bytes 294912 | tf_op jit(solution)/shard_map/all_gather | solution.py:11
  19.1 0.0 copy-done
  19.1 4.1 %convolution_convert_fusion = bf16[2048,1024]{1,0:T(8,128)(2,1)} fusion(bf16[2048,128]{1,0:T(8,128)(2,1)S(1)} %bitcast.47, bf16[1024,128]{1,0:T(8,128)(2,1)} %param.7), kind=kOutput, calls=%fused_computation.2 | convolution fusion | flops 538968064 | bytes 4980736 | tf_op jit(solution)/shard_map/dot_general | solution.py:23
  23.2 6.5 %copy.17 = bf16[2048,1024]{0,1:T(8,128)(2,1)} copy(bf16[2048,1024]{1,0:T(8,128)(2,1)} %convolution_convert_fusion) | data formatting | bytes 8388608 | tf_op jit(solution)/shard_map/convert_element_type | solution.py:26
  29.7 12.9 %reshape.16 = bf16[32,64,32,32]{1,0,3,2:T(8,128)(2,1)} reshape(bf16[2048,1024]{0,1:T(8,128)(2,1)} %copy.17) | data formatting | bytes 8388608 | tf_op jit(solution)/shard_map/reshape | solution.py:26
  42.6 0.0 copy-start.1
  42.6 5.7 %fusion.4 = f32[32,64,32]{1,2,0:T(8,128)S(1)} fusion(bf16[32,64,32,32]{1,0,3,2:T(8,128)(2,1)} %reshape.16, bf16[32,64,64]{2,1,0:T(8,128)(2,1)S(1)} %all_gather.12), kind=kOutput, calls=%fused_computation.8 | convolution fusion | flops 268500992 | bytes 4718592 | tf_op jit(solution)/shard_map/ijcd,dsj->csi/dot_general | solution.py:28
  48.3 1.9 %copy.18 = f32[32,64,32]{2,0,1:T(8,128)} copy(f32[32,64,32]{1,2,0:T(8,128)S(1)} %fusion.4) | data formatting | bytes 524288 | tf_op jit(solution)/shard_map/div | solution.py:28
  50.2 0.0 reduce-scatter.4.cloned.1.call-update
  50.2 0.0 reduce-scatter.8.cloned.1.call-start
  50.2 0.0 copy-done.1
  50.2 22.2 %all_gather.13 = bf16[32,64,32]{2,1,0:T(8,128)(2,1)S(1)} all-gather(bf16[32,16,32]{2,1,0:T(8,128)(2,1)S(1)} %copy-done.1), channel_id=1, replica_groups=mesh['row'=8,'col'=4] {'col'}, dimensions={1}, use_global_device_ids=true | all-gather | bytes 163840 | tf_op jit(solution)/shard_map/all_gather | solution.py:10
  72.4 5.6 %fusion = bf16[32,64,32,32]{1,0,2,3:T(8,128)(2,1)} fusion(bf16[32,64,64]{2,1,0:T(8,128)(2,1)S(1)} %all_gather.12, bf16[32,64,32]{2,1,0:T(8,128)(2,1)S(1)} %all_gather.13), kind=kOutput, calls=%fused_computation.1 | convolution fusion | flops 272629760 | bytes 4587520 | tf_op jit(solution)/shard_map/csi,dsj->ijcd/dot_general | solution.py:15
  78.0 9.2 %copy.20 = bf16[32,64,32,32]{1,0,3,2:T(8,128)(2,1)} copy(bf16[32,64,32,32]{1,0,2,3:T(8,128)(2,1)} %fusion) | data formatting | bytes 8388608 | tf_op jit(solution)/shard_map/convert_element_type | solution.py:16
  87.2 12.3 %reshape.17 = bf16[2048,1024]{0,1:T(8,128)(2,1)} reshape(bf16[32,64,32,32]{1,0,3,2:T(8,128)(2,1)} %copy.20) | data formatting | bytes 8388608 | tf_op jit(solution)/shard_map/reshape | solution.py:17
  99.5 4.2 %fusion.9 = f32[1024,128]{1,0:T(8,128)} fusion(bf16[2048,1024]{0,1:T(8,128)(2,1)} %reshape.17, bf16[2048,128]{1,0:T(8,128)(2,1)S(1)} %bitcast.48), kind=kOutput, calls=%fused_computation.13 | convolution fusion | flops 536870912 | bytes 5242880 | tf_op jit(solution)/shard_map/dot_general | solution.py:20
  103.8 0.0 reduce-scatter.8.cloned.1.call-update
  103.8 0.2 reduce-scatter.6.cloned.1.call-start
  104.0 7.0 %fusion.2 = f32[32,64,64]{1,2,0:T(8,128)S(1)} fusion(bf16[32,64,32,32]{1,0,3,2:T(8,128)(2,1)} %reshape.16, bf16[32,64,32]{2,1,0:T(8,128)(2,1)S(1)} %all_gather.13), kind=kOutput, calls=%fused_computation.5 | convolution fusion | flops 268566528 | bytes 4849664 | tf_op jit(solution)/shard_map/ijcd,csi->dsj/dot_general | solution.py:31
  111.1 1.8 copy.19
  112.8 0.0 reduce-scatter.6.cloned.1.call-update
  112.9 0.0 reduce-scatter.4.cloned.1.call-done
  112.9 1.8 copy.21
  114.7 22.1 %reduce-scatter.8.cloned.1.call-done = f32[128,128]{1,0:T(8,128)} async-done(((f32[1024,128]{1,0:T(8,128)}), f32[128,128]{1,0:T(8,128)}) %reduce-scatter.8.cloned.1.call-update) | async-done | bytes 65552 | tf_op jit(solution)/shard_map/reduce_scatter | solution.py:21
  136.8 14.1 %all-gather = f32[512,128]{1,0:T(8,128)S(1)} all-gather(f32[128,128]{1,0:T(8,128)} %reduce-scatter.8.cloned.1.call-done), channel_id=2, replica_groups=mesh['row'=8,'col'=4] {'col'}, dimensions={0}, use_global_device_ids=true | all-gather | bytes 327680 | tf_op jit(solution)/shard_map/all_gather | solution.py:22
  150.9 0.6 reduce_sum.9
  151.5 24.4 %reduce-scatter.6.cloned.1.call-done = f32[32,8,64]{2,0,1:T(8,128)} async-done(((f32[32,64,64]{2,0,1:T(8,128)}), f32[32,8,64]{2,0,1:T(8,128)}) %reduce-scatter.6.cloned.1.call-update) | async-done | bytes 65552 | tf_op jit(solution)/shard_map/reduce_scatter | solution.py:34
  176.0 1.6 copy.22
Async XLA Ops:
  7.2 12.0 %copy-start = (bf16[32,64,128]{2,1,0:T(8,128)(2,1)S(1)}, bf16[32,64,128]{2,1,0:T(8,128)(2,1)}, u32[]{:S(2)}) copy-start(bf16[32,64,128]{2,1,0:T(8,128)(2,1)} %param.6) | copy-start | bytes 1572868
  7.2 105.7 %reduce-scatter.4.cloned.1.call-start = ((), (), s32[]{:S(2)}) async-start(), calls=%async_computation.3 | async-start | bytes 1310720 | tf_op jit(solution)/shard_map/reduce_scatter | solution.py:33
  42.6 7.7 %copy-start.1 = (bf16[32,16,32]{2,1,0:T(8,128)(2,1)S(1)}, bf16[32,16,32]{2,1,0:T(8,128)(2,1)}, u32[]{:S(2)}) copy-start(bf16[32,16,32]{2,1,0:T(8,128)(2,1)} %param.4) | copy-start | bytes 98308
  50.2 86.6 %reduce-scatter.8.cloned.1.call-start = ((), (), s32[]{:S(2)}) async-start(), calls=%async_computation.5 | async-start | bytes 589824 | tf_op jit(solution)/shard_map/reduce_scatter | solution.py:21
  103.8 72.2 %reduce-scatter.6.cloned.1.call-start = ((), (), s32[]{:S(2)}) async-start(), calls=%async_computation.4 | async-start | bytes 1179648 | tf_op jit(solution)/shard_map/reduce_scatter | solution.py:34
Sparse Core Ops, SparseCore 0:
  50.3 32.7 reduce-scatter.3
  103.9 32.8 reduce-scatter.7
  139.9 35.9 reduce-scatter.5
